TPU v7x, 32 devices: a whole 2x2x4 slice. The times are simulated.
32 devices in a mesh: row: 8 (over z, y), col: 4 (over x, core).
Axes of the slice: x: 2, y: 2, z: 4, core: 2. Of those that a mesh axis runs over, the one named last changes fastest.
Arguments:
- momentum: float32 [8192, 16384], P('row', 'col'), may hold values from -6 to 6
- grads: bfloat16 [2, 8192, 16384], P(None, 'row', 'col'), may hold values from -400 to 400
- basis: float32 [16384, 256], P('col'), may hold values from -0.046875 to 0.046875
Outputs:
- change: bfloat16 [8192, 16384], P('row', 'col')
- state: float32 [8192, 16384], P('row', 'col')
All inputs are finite; a program needn't handle non-finite values.
Results may differ from a plain program's by a relative error of at most 0.0035.
Values sent between devices are 32-bit elements; how exact they have to be, the bound alone decides.
A program may use at most 192 MiB of HBM per device.

v0:
```python
import jax
import jax.numpy as jnp
from jax import lax
from jax.sharding import PartitionSpec as P

ROWS = 8192
COLS = 16384
RANK = 256
STEPS = 2


keep_rate = 0.95
norm_eps = 1e-06


def column_squares(matrix):
    return jnp.sum(matrix * matrix, axis=0)


def shards(momentum, grads, basis):
    high = lax.Precision.HIGHEST
    factor = (ROWS * COLS / RANK) ** 0.5
    state = momentum
    right = basis
    change = jnp.zeros(momentum.shape, jnp.float32)
    for step in range(STEPS):
        buffer = state + grads[step].astype(jnp.float32)
        partial_value = jnp.dot(buffer, right, precision=high, preferred_element_type=jnp.float32)
        projected = lax.psum(partial_value, "col")
        gram = lax.psum(
            jnp.dot(projected.T, projected, precision=high, preferred_element_type=jnp.float32),
            "row",
        )
        lower = jnp.linalg.cholesky(gram)
        ortho = jax.scipy.linalg.solve_triangular(lower, projected.T, lower=True).T
        local_right = lax.dot_general(
            buffer,
            ortho,
            (((0,), (0,)), ((), ())),
            precision=high,
            preferred_element_type=jnp.float32,
        )
        raw = lax.psum(local_right, "row")
        squares = lax.psum(column_squares(raw), "col")
        right = raw * lax.rsqrt(squares + norm_eps)
        state = buffer - (1.0 - keep_rate) * jnp.dot(
            ortho, raw.T, precision=high, preferred_element_type=jnp.float32
        )
        change = change + factor * jnp.dot(
            ortho, right.T, precision=high, preferred_element_type=jnp.float32
        )
    return (change.astype(jnp.bfloat16), state)


def solution(mesh):
    return jax.shard_map(
        shards,
        mesh=mesh,
        in_specs=(P("row", "col"), P(None, "row", "col"), P("col", None)),
        out_specs=(P("row", "col"), P("row", "col")),
        check_vma=False,
    )
```

profile of v0, /device:TPU:0, one launch (start us, length us, event | category | flops | bytes accessed | tf_op | source)
XLA Modules:
  0.0 904.7 jit_solution(4281090039093472297)
XLA Ops:
  7.2 20.3 %fusion.1 = f32[1024,256]{1,0:T(8,128)} fusion(f32[4096,256]{1,0:T(8,128)} %param.8, f32[1024,4096]{1,0:T(8,128)} %param.6, bf16[2,1024,4096]{2,1,0:T(8,128)(2,1)} %param.7), kind=kOutput, calls=%fused_computation.9 | convolution fusion | flops 12893290496 | bytes 30408704 | tf_op jit(solution)/shard_map/dot_general | solution.py:28
  27.6 39.1 %all-reduce.8.cloned.1.call-done = f32[1024,256]{1,0:T(8,128)} async-done(((f32[1024,256]{1,0:T(8,128)}), f32[1024,256]{1,0:T(8,128)}) %all-reduce.8.cloned.1.call-update) | async-done | bytes 1048592 | tf_op jit(solution)/shard_map/psum | solution.py:29
  71.0 71.4 %all-reduce.10.cloned.1.call-done = f32[256,256]{0,1:T(8,128)} async-done(((f32[256,256]{0,1:T(8,128)}), f32[256,256]{0,1:T(8,128)}) %all-reduce.10.cloned.1.call-update) | async-done | bytes 262160 | tf_op jit(solution)/shard_map/psum | solution.py:30
  144.5 11.7 %cholesky.130 = f32[128,128]{1,0:T(8,128)S(1)} custom-call(f32[128,128]{1,0:T(8,128)S(1)} %cholesky.194), custom_call_target="Cholesky" | custom-call | tf_op jit(solution)/shard_map/jit(cholesky)/cholesky | solution.py:34
  156.3 9.8 %custom-call.13 = f32[1,128,128]{1,2,0:T(8,128)S(1)} custom-call(f32[1,128,128]{2,1,0:T(8,128)S(1)} %get-tuple-element.47), custom_call_target="InvertDiagBlocksLowerTriangular" | custom-call | tf_op jit(solution)/shard_map/jit(cholesky)/cholesky | solution.py:34
  166.6 11.7 %cholesky.147 = f32[128,128]{1,0:T(8,128)S(1)} custom-call(f32[128,128]{1,0:T(8,128)S(1)} %convolution_subtract_fusion.3), custom_call_target="Cholesky" | custom-call | tf_op jit(solution)/shard_map/jit(cholesky)/cholesky | solution.py:34
  184.6 19.7 %custom-call.14 = f32[2,128,128]{1,2,0:T(8,128)S(1)} custom-call(f32[2,128,128]{2,1,0:T(8,128)S(1)} %get-tuple-element.18), custom_call_target="InvertDiagBlocksLowerTriangular" | custom-call | tf_op jit(solution)/shard_map/jit(_solve_triangular)/triangular_solve | solution.py:35
  208.7 32.9 %fusion = f32[4096,256]{1,0:T(8,128)} fusion(f32[1024,4096]{1,0:T(8,128)} %param.6, bf16[2,1024,4096]{2,1,0:T(8,128)(2,1)} %param.7, f32[128,1024]{1,0:T(8,128)S(1)} %fusion.22, f32[128,1024]{1,0:T(8,128)S(1)} %fusion.13), kind=kOutput, calls=%fused_computation.8 | convolution fusion | flops 12893552640 | bytes 30408704 | tf_op jit(solution)/shard_map/dot_general | solution.py:36
  241.7 155.7 %all-reduce.12.cloned.1.call-done = f32[4096,256]{1,0:T(8,128)} async-done(((f32[4096,256]{1,0:T(8,128)}), f32[4096,256]{1,0:T(8,128)}) %all-reduce.12.cloned.1.call-update) | async-done | bytes 4194320 | tf_op jit(solution)/shard_map/psum | solution.py:43
  400.1 6.4 psum.59
  406.5 36.7 %convert_add_fusion = f32[1024,4096]{1,0:T(8,128)} fusion(f32[4096,256]{1,0:T(8,128)} %all-reduce.12.cloned.1.call-done, bf16[2,1024,4096]{2,1,0:T(8,128)(2,1)} %param.7, f32[1024,4096]{1,0:T(8,128)} %param.6, f32[128,1024]{1,0:T(8,128)S(1)} %fusion.22, f32[128,1024]{1,0:T(8,128)S(1)} %fusion.13), kind=kOutput, calls=%fused_computation.4 | convolution fusion | flops 12910329856 | bytes 55574528 | tf_op jit(solution)/shard_map/dot_general | solution.py:46
  443.3 17.2 %fusion.3 = f32[1024,256]{1,0:T(8,128)} fusion(f32[1024,4096]{1,0:T(8,128)} %convert_add_fusion, f32[4096,256]{1,0:T(8,128)} %all-reduce.12.cloned.1.call-done, f32[256]{0:T(256)S(1)} %add_rsqrt_fusion.1), kind=kOutput, calls=%fused_computation.13 | convolution fusion | flops 12885950464 | bytes 22021120 | tf_op jit(solution)/shard_map/dot_general | solution.py:28
  460.8 34.7 %all-reduce.14.cloned.1.call-done = f32[1024,256]{1,0:T(8,128)} async-done(((f32[1024,256]{1,0:T(8,128)}), f32[1024,256]{1,0:T(8,128)}) %all-reduce.14.cloned.1.call-update) | async-done | bytes 1048592 | tf_op jit(solution)/shard_map/psum | solution.py:29
  499.6 71.6 %all-reduce.16.cloned.1.call-done = f32[256,256]{0,1:T(8,128)} async-done(((f32[256,256]{0,1:T(8,128)}), f32[256,256]{0,1:T(8,128)}) %all-reduce.16.cloned.1.call-update) | async-done | bytes 262160 | tf_op jit(solution)/shard_map/psum | solution.py:30
  573.3 11.7 %cholesky.164 = f32[128,128]{1,0:T(8,128)S(1)} custom-call(f32[128,128]{1,0:T(8,128)S(1)} %cholesky.197), custom_call_target="Cholesky" | custom-call | tf_op jit(solution)/shard_map/jit(cholesky)/cholesky | solution.py:34
  585.7 9.8 %custom-call.15 = f32[1,128,128]{1,2,0:T(8,128)S(1)} custom-call(f32[1,128,128]{2,1,0:T(8,128)S(1)} %get-tuple-element.43), custom_call_target="InvertDiagBlocksLowerTriangular" | custom-call | tf_op jit(solution)/shard_map/jit(cholesky)/cholesky | solution.py:34
  596.0 11.7 %cholesky.181 = f32[128,128]{1,0:T(8,128)S(1)} custom-call(f32[128,128]{1,0:T(8,128)S(1)} %convolution_subtract_fusion.2), custom_call_target="Cholesky" | custom-call | tf_op jit(solution)/shard_map/jit(cholesky)/cholesky | solution.py:34
  614.4 19.7 %custom-call.16 = f32[2,128,128]{1,2,0:T(8,128)S(1)} custom-call(f32[2,128,128]{2,1,0:T(8,128)S(1)} %get-tuple-element.19), custom_call_target="InvertDiagBlocksLowerTriangular" | custom-call | tf_op jit(solution)/shard_map/jit(_solve_triangular)/triangular_solve | solution.py:35
  638.5 29.9 %fusion.10 = f32[4096,256]{1,0:T(8,128)} fusion(f32[1024,4096]{1,0:T(8,128)} %convert_add_fusion, f32[128,1024]{1,0:T(8,128)S(1)} %fusion.18, f32[128,1024]{1,0:T(8,128)S(1)} %fusion.11), kind=kOutput, calls=%fused_computation.26 | convolution fusion | flops 12885164032 | bytes 22020096 | tf_op jit(solution)/shard_map/dot_general | solution.py:36
  668.4 30.2 %fusion.5 = f32[1024,4096]{1,0:T(8,128)} fusion(f32[4096,256]{1,0:T(8,128)} %all-reduce.12.cloned.1.call-done, f32[256]{0:T(256)S(1)} %add_rsqrt_fusion.1, f32[128,1024]{1,0:T(8,128)S(1)} %fusion.22, f32[128,1024]{1,0:T(8,128)S(1)} %fusion.13), kind=kOutput, calls=%fused_computation.15 | convolution fusion | flops 12886212608 | bytes 22021120 | tf_op jit(solution)/shard_map/dot_general | solution.py:49
  698.5 125.6 %all-reduce.18.cloned.1.call-done = f32[4096,256]{1,0:T(8,128)} async-done(((f32[4096,256]{1,0:T(8,128)}), f32[4096,256]{1,0:T(8,128)}) %all-reduce.18.cloned.1.call-update) | async-done | bytes 4194320 | tf_op jit(solution)/shard_map/psum | solution.py:43
  826.9 6.6 psum.63
  833.5 33.4 %multiply_subtract_fusion = f32[1024,4096]{1,0:T(8,128)} fusion(f32[1024,4096]{1,0:T(8,128)} %convert_add_fusion, f32[4096,256]{1,0:T(8,128)} %all-reduce.18.cloned.1.call-done, f32[128,1024]{1,0:T(8,128)S(1)} %fusion.18, f32[128,1024]{1,0:T(8,128)S(1)} %fusion.11), kind=kOutput, calls=%fused_computation.7 | convolution fusion | flops 12893552640 | bytes 38797312 | tf_op jit(solution)/shard_map/dot_general | solution.py:46
  866.9 30.6 %multiply_convert_fusion = bf16[1024,4096]{1,0:T(8,128)(2,1)} fusion(f32[1024,4096]{1,0:T(8,128)} %fusion.5, f32[4096,256]{1,0:T(8,128)S(1)} %copy-done, f32[256]{0:T(256)S(1)} %add_rsqrt_fusion, f32[128,1024]{1,0:T(8,128)S(1)} %fusion.18, f32[128,1024]{1,0:T(8,128)S(1)} %fusion.11), kind=kOutput, calls=%fused_computation.6 | convolution fusion | flops 12898795520 | bytes 30409728 | tf_op jit(solution)/shard_map/dot_general | solution.py:49
  (65 shorter events, 47.3 us)
Async XLA Ops:
  7.2 59.5 %all-reduce.8.cloned.1.call-start = ((), (), s32[]{:S(2)}) async-start(), calls=%async_computation | async-start | bytes 2097152 | tf_op jit(solution)/shard_map/psum | solution.py:29
  27.5 114.9 %all-reduce.10.cloned.1.call-start = ((), (), s32[]{:S(2)}) async-start(), calls=%async_computation.1 | async-start | bytes 524288 | tf_op jit(solution)/shard_map/psum | solution.py:30
  70.8 326.6 %all-reduce.12.cloned.1.call-start = ((), (), s32[]{:S(2)}) async-start(), calls=%async_computation.2 | async-start | bytes 8388608 | tf_op jit(solution)/shard_map/psum | solution.py:43
  241.6 253.9 %all-reduce.14.cloned.1.call-start = ((), (), s32[]{:S(2)}) async-start(), calls=%async_computation.3 | async-start | bytes 2097152 | tf_op jit(solution)/shard_map/psum | solution.py:29
  460.5 110.7 %all-reduce.16.cloned.1.call-start = ((), (), s32[]{:S(2)}) async-start(), calls=%async_computation.4 | async-start | bytes 524288 | tf_op jit(solution)/shard_map/psum | solution.py:30
  499.6 324.5 %all-reduce.18.cloned.1.call-start = ((), (), s32[]{:S(2)}) async-start(), calls=%async_computation.5 | async-start | bytes 8388608 | tf_op jit(solution)/shard_map/psum | solution.py:43
  833.5 33.5 %copy-start = (f32[4096,256]{1,0:T(8,128)S(1)}, f32[4096,256]{1,0:T(8,128)}, u32[]{:S(2)}) copy-start(f32[4096,256]{1,0:T(8,128)} %all-reduce.18.cloned.1.call-done) | copy-start | bytes 12582916
Sparse Core Ops, SparseCore 0:
  27.7 39.0 all-reduce.7
  70.9 71.4 all-reduce.9
  241.8 155.5 all-reduce.11
  460.7 34.8 all-reduce.13
  499.7 71.4 all-reduce.15
  668.5 155.5 all-reduce.17
where the time goes:
time: 911 us; the launch traced here: 905 us
  waiting for transfers between devices  498 us (55%)
  matrix products  249 us (27%)
  other arithmetic  116 us (13%)
  between operations  17.3 us (2%)
  blocking collectives  13 us (1%)
  local copies, waits for them, and re-layouts  10.4 us (1%)
    psum x2, waiting for transfers between devices, shards(): raw = lax.psum(local_right, 'row')  281 us
    psum x2, waiting for transfers between devices, shards(): lax.psum(jnp.dot(projected.T, projected, precision=high, preferred_elemen...  143 us
    psum x2, waiting for transfers between devices, shards(): projected = lax.psum(partial_value, 'col')  73.8 us
    dot_general x2, matrix products, shards(): jnp.dot(ortho, raw.T, precision=high, preferred_element_type=jnp.float32)  70.2 us
    another operation x13, other arithmetic, shards(): lower = jnp.linalg.cholesky(gram)  68.7 us
    dot_general x2, matrix products, shards(): lax.dot_general(buffer, ortho, (((0,), (0,)), ((), ())), precision=high,...  62.8 us
    dot_general x2, matrix products, shards(): jnp.dot(ortho, right.T, precision=high, preferred_element_type=jnp.float32)  60.8 us
    another operation x5, other arithmetic, shards(): ortho = jax.scipy.linalg.solve_triangular(lower, projected.T, lower=True).T  39.4 us
  transfers between devices with their start and end apart: 6, of which 6 were waited for; matrix products, arithmetic and copies ran while one was open for 3% of the time, Pallas kernels for 0%

commit v1 on v0

v1 whole, which is shorter than its diff:
```python
import functools

import jax
import jax.numpy as jnp
from jax import lax
from jax.experimental import pallas as pl
from jax.experimental.pallas import tpu as pltpu
from jax.sharding import PartitionSpec as P

keep_rate = 0.95
norm_eps = 1e-06
HIGH = lax.Precision.HIGH
HIGHEST = lax.Precision.HIGHEST


def matmul(a, b, dims, precision):
    return lax.dot_general(a, b, (dims, ((), ())), precision=precision, preferred_element_type=jnp.float32)


def reduce_kernel(axis, bits, count, *refs):
    inputs, outs, recvs, works = (refs[k * count : (k + 1) * count] for k in range(4))
    send_sem, recv_sem = refs[4 * count :]
    me = lax.axis_index(axis)
    halves = [lax.rem(me // (1 << b), 2) for b in bits]
    partners = [me + (1 - 2 * h) * (1 << b) for h, b in zip(halves, bits)]
    barrier = pltpu.get_barrier_semaphore()
    for p in partners:
        pl.semaphore_signal(barrier, inc=1, device_id={axis: p}, device_id_type=pl.DeviceIdType.MESH)
    pl.semaphore_wait(barrier, len(bits))

    starts = [[0] for _ in range(count)]
    for s in range(len(bits)):
        copies = []
        for i in range(count):
            size = inputs[i].shape[0] >> (s + 1)
            base = inputs[i].shape[0] - 2 * size
            source = inputs[i] if s == 0 else works[i]
            there = pl.multiple_of(starts[i][s] + (1 - halves[s]) * size, 8)
            copy = pltpu.make_async_remote_copy(
                src_ref=source.at[pl.ds(there, size)],
                dst_ref=recvs[i].at[pl.ds(base, size)],
                send_sem=send_sem.at[i, s],
                recv_sem=recv_sem.at[i, s],
                device_id={axis: partners[s]},
                device_id_type=pl.DeviceIdType.MESH,
            )
            copy.start()
            copies.append(copy)
        for i in range(count):
            size = inputs[i].shape[0] >> (s + 1)
            base = inputs[i].shape[0] - 2 * size
            source = inputs[i] if s == 0 else works[i]
            here = pl.multiple_of(starts[i][s] + halves[s] * size, 8)
            copies[i].wait()
            target = outs[i] if s == len(bits) - 1 else works[i]
            target[pl.ds(here, size), :] = source[pl.ds(here, size), :] + recvs[i][pl.ds(base, size), :]
            starts[i].append(here)
    for s in reversed(range(len(bits))):
        t = 2 * len(bits) - 1 - s
        copies = []
        for i in range(count):
            size = inputs[i].shape[0] >> (s + 1)
            mine = outs[i].at[pl.ds(starts[i][s + 1], size)]
            copy = pltpu.make_async_remote_copy(
                src_ref=mine,
                dst_ref=mine,
                send_sem=send_sem.at[i, t],
                recv_sem=recv_sem.at[i, t],
                device_id={axis: partners[s]},
                device_id_type=pl.DeviceIdType.MESH,
            )
            copy.start()
            copies.append(copy)
        for copy in copies:
            copy.wait()


def all_reduce(arrays, axis, size, collective_id):
    bits = list(range(size.bit_length() - 1))
    count = len(arrays)
    total = sum(a.size for a in arrays)
    vmem = pl.BlockSpec(memory_space=pltpu.VMEM)
    return pl.pallas_call(
        functools.partial(reduce_kernel, axis, bits, count),
        out_shape=[jax.ShapeDtypeStruct(a.shape, a.dtype) for a in arrays],
        in_specs=[vmem] * count,
        out_specs=[vmem] * count,
        scratch_shapes=[pltpu.VMEM(a.shape, a.dtype) for a in arrays * 2]
        + [pltpu.SemaphoreType.DMA((count, 2 * len(bits))), pltpu.SemaphoreType.DMA((count, 2 * len(bits)))],
        compiler_params=pltpu.CompilerParams(
            collective_id=collective_id, has_side_effects=True, vmem_limit_bytes=16 * 2**20
        ),
        cost_estimate=pl.CostEstimate(flops=total, bytes_accessed=40 * total, transcendentals=0),
    )(*arrays)


def shards(row_size, col_size, momentum, grads, basis):
    rank = basis.shape[1]
    factor = (momentum.shape[0] * row_size * momentum.shape[1] * col_size / rank) ** 0.5
    eye = jnp.eye(rank, dtype=jnp.float32)
    state = momentum
    right = basis
    scale = None
    squares = None
    lefts, rights = [], []
    steps = grads.shape[0]
    for step in range(steps):
        buffer = state + grads[step].astype(jnp.float32)
        partial_value = matmul(buffer, right, ((1,), (0,)), HIGH)
        if step == 0:
            (projected,) = all_reduce([partial_value], "col", col_size, 0)
        else:
            projected, squares = all_reduce([partial_value, squares], "col", col_size, 1)
            scale = lax.rsqrt(squares[:1] + norm_eps)
            projected = projected * scale
            rights.append(right * scale)
        product = lax.psum(matmul(buffer, projected, ((0,), (0,)), HIGH), "row")
        part = matmul(projected, projected, ((0,), (0,)), HIGHEST)
        (gram,) = all_reduce([part], "row", row_size, 2)
        lower = jnp.linalg.cholesky(gram)
        inverse = jax.scipy.linalg.solve_triangular(lower, eye, lower=True)
        ortho = matmul(projected, inverse, ((1,), (1,)), HIGHEST)
        raw = matmul(product, inverse, ((1,), (1,)), HIGHEST)
        lefts.append(ortho)
        squares = jnp.pad(jnp.sum(raw * raw, axis=0, keepdims=True), ((0, 8 * col_size - 1), (0, 0)))
        right = raw
        state = buffer - (1.0 - keep_rate) * matmul(
            ortho.astype(jnp.bfloat16), raw.astype(jnp.bfloat16), ((1,), (1,)), None
        )
    (squares,) = all_reduce([squares], "col", col_size, 3)
    rights.append(right * lax.rsqrt(squares[:1] + norm_eps))
    change = factor * matmul(jnp.concatenate(lefts, 1), jnp.concatenate(rights, 1), ((1,), (1,)), HIGH)
    return (change.astype(jnp.bfloat16), state)


def solution(mesh):
    return jax.shard_map(
        functools.partial(shards, mesh.shape["row"], mesh.shape["col"]),
        mesh=mesh,
        in_specs=(P("row", "col"), P(None, "row", "col"), P("col", None)),
        out_specs=(P("row", "col"), P("row", "col")),
        check_vma=False,
    )
```

time: 911 us -> 532 us (0.58)
  waiting for transfers between devices: 498 us -> 111 us
  Pallas kernels: 0 us -> 128 us
  matrix products: 249 us -> 144 us
  blocking collectives: 13 us -> 0 us
    psum x6 -> x2, waiting for transfers between devices: 498 us -> 111 us  [shards(): product = lax.psum(matmul(buffer, projected, ((0,), (0,)), HIGH), 'row')]
    pallas_call x0 -> x5, Pallas kernels: none -> 128 us  [all_reduce(): pl.pallas_call(functools.partial(reduce_kernel, axis, bits, count), out_s...]
    dot_general x10 -> x13, matrix products: 239 us -> 141 us  [matmul(): lax.dot_general(a, b, (dims, ((), ())), precision=precision, preferred_el...]
    psum x2 -> x0, blocking collectives: 13 us -> none  [shards(): squares = lax.psum(column_squares(raw), 'col')]
  transfers between devices with their start and end apart: 6 -> 2, of which waited for: 6 -> 2; matrix products, arithmetic and copies ran while one was open for 3% -> 25% of each run, Pallas kernels for 0% -> 15%
where the time goes in v1:
time: 532 us; the launch traced here: 524 us
  matrix products  144 us (27%)
  Pallas kernels  128 us (24%)
  other arithmetic  113 us (21%)
  waiting for transfers between devices  111 us (21%)
  between operations  17.3 us (3%)
  local copies, waits for them, and re-layouts  9.94 us (2%)
    dot_general x13, matrix products, matmul(): lax.dot_general(a, b, (dims, ((), ())), precision=precision, preferred_el...  141 us
    pallas_call x5, Pallas kernels, all_reduce(): pl.pallas_call(functools.partial(reduce_kernel, axis, bits, count), out_s...  128 us
    psum x2, waiting for transfers between devices, shards(): product = lax.psum(matmul(buffer, projected, ((0,), (0,)), HIGH), 'row')  111 us
    another operation x13, other arithmetic, shards(): lower = jnp.linalg.cholesky(gram)  69 us
    another operation x5, other arithmetic, shards(): inverse = jax.scipy.linalg.solve_triangular(lower, eye, lower=True)  39.4 us
  transfers between devices with their start and end apart: 2, of which 2 were waited for; matrix products, arithmetic and copies ran while one was open for 25% of the time, Pallas kernels for 15%

profile of v1, /device:TPU:0, one launch (start us, length us, event | category | flops | bytes accessed | tf_op | source)
XLA Modules:
  0.0 524.1 jit_solution(12639653411834808968)
XLA Ops:
  7.2 13.1 %fusion.4.refs_0_ = f32[1024,256]{1,0:T(8,128)S(1)} fusion(f32[4096,256]{1,0:T(8,128)} %param.8, f32[1024,4096]{1,0:T(8,128)} %param.6, bf16[2,1024,4096]{2,1,0:T(8,128)(2,1)} %param.7), kind=kOutput, calls=%fused_computation.12 | convolution fusion | flops 6450839552 | bytes 30408704 | tf_op jit(solution)/shard_map/dot_general | solution.py:17
  20.4 21.3 %shard_map.50 = f32[1024,256]{1,0:T(8,128)S(1)} custom-call(f32[1024,256]{1,0:T(8,128)S(1)} %fusion.4.refs_0_), custom_call_target="tpu_custom_call" | custom-call | flops 262144 | bytes 10485760 | tf_op jit(solution)/shard_map/pallas_call | solution.py:83
  41.7 20.0 %fusion.3 = f32[4096,256]{1,0:T(8,128)} fusion(f32[1024,256]{1,0:T(8,128)S(1)} %shard_map.50, f32[1024,4096]{1,0:T(8,128)} %param.6, bf16[2,1024,4096]{2,1,0:T(8,128)(2,1)} %param.7), kind=kOutput, calls=%fused_computation.11 | convolution fusion | flops 6450839552 | bytes 30408704 | tf_op jit(solution)/shard_map/dot_general | solution.py:17
  63.8 39.9 %shard_map.51 = f32[256,256]{1,0:T(8,128)S(1)} custom-call(f32[256,256]{1,0:T(8,128)S(1)} %fusion.48.refs_0_), custom_call_target="tpu_custom_call" | custom-call | flops 65536 | bytes 2621440 | tf_op jit(solution)/shard_map/pallas_call | solution.py:83
  103.9 11.7 %cholesky.130 = f32[128,128]{1,0:T(8,128)S(1)} custom-call(f32[128,128]{1,0:T(8,128)S(1)} %cholesky.194), custom_call_target="Cholesky" | custom-call | tf_op jit(solution)/shard_map/jit(cholesky)/cholesky | solution.py:120
  115.6 9.8 %custom-call.13 = f32[1,128,128]{1,2,0:T(8,128)S(1)} custom-call(f32[1,128,128]{2,1,0:T(8,128)S(1)} %get-tuple-element.51), custom_call_target="InvertDiagBlocksLowerTriangular" | custom-call | tf_op jit(solution)/shard_map/jit(cholesky)/cholesky | solution.py:120
  126.0 11.7 %cholesky.147 = f32[128,128]{1,0:T(8,128)S(1)} custom-call(f32[128,128]{1,0:T(8,128)S(1)} %convolution_subtract_fusion.3), custom_call_target="Cholesky" | custom-call | tf_op jit(solution)/shard_map/jit(cholesky)/cholesky | solution.py:120
  143.9 19.7 %custom-call.14 = f32[2,128,128]{1,2,0:T(8,128)S(1)} custom-call(f32[2,128,128]{2,1,0:T(8,128)S(1)} %get-tuple-element.22), custom_call_target="InvertDiagBlocksLowerTriangular" | custom-call | tf_op jit(solution)/shard_map/jit(_solve_triangular)/triangular_solve | solution.py:121
  165.5 57.8 %all-reduce.6.cloned.1.call-done = f32[4096,256]{1,0:T(8,128)} async-done(((f32[4096,256]{1,0:T(8,128)}), f32[4096,256]{1,0:T(8,128)}) %all-reduce.6.cloned.1.call-update) | async-done | bytes 4194320 | tf_op jit(solution)/shard_map/psum | solution.py:117
  223.4 7.7 %multiply_reduce_fusion.1 = (f32[256]{0:T(256)S(1)}, f32[4096,256]{1,0:T(8,128)}) fusion(f32[4096,256]{1,0:T(8,128)} %all-reduce.6.cloned.1.call-done, f32[128,256]{1,0:T(8,128)S(1)} %fusion.36, f32[128,256]{1,0:T(8,128)S(1)} %fusion.29), kind=kOutput, calls=%fused_computation.14 | convolution fusion | flops 3223387904 | bytes 8651776 | tf_op jit(solution)/shard_map/dot_general | solution.py:17
  231.0 17.7 %convert_add_fusion = f32[1024,4096]{1,0:T(8,128)} fusion(bf16[2,1024,4096]{2,1,0:T(8,128)(2,1)} %param.7, f32[1024,4096]{1,0:T(8,128)} %param.6, f32[4096,256]{1,0:T(8,128)} %get-tuple-element.55, f32[1024,256]{0,1:T(8,128)S(1)} %fusion.26), kind=kOutput, calls=%fused_computation.4 | convolution fusion | flops 2173960192 | bytes 55574528 | tf_op jit(solution)/shard_map/dot_general | solution.py:17
  248.8 12.9 %fusion.49.refs_0_ = f32[1024,256]{1,0:T(8,128)S(1)} fusion(f32[1024,4096]{1,0:T(8,128)} %convert_add_fusion, f32[4096,256]{1,0:T(8,128)} %get-tuple-element.55), kind=kOutput, calls=%fused_computation.96 | convolution fusion | flops 6442450944 | bytes 22020096 | tf_op jit(solution)/shard_map/dot_general | solution.py:17
  261.7 20.3 %shard_map.52 = (f32[1024,256]{1,0:T(8,128)S(1)}, f32[32,256]{1,0:T(8,128)S(1)}) custom-call(f32[1024,256]{1,0:T(8,128)S(1)} %fusion.49.refs_0_, f32[32,256]{1,0:T(8,128)S(1)} %pad.8.refs_1_), custom_call_target="tpu_custom_call" | custom-call | flops 270336 | bytes 10813440 | tf_op jit(solution)/shard_map/pallas_call | solution.py:83
  282.0 15.6 %fusion.10 = f32[4096,256]{1,0:T(8,128)} fusion(f32[1024,4096]{1,0:T(8,128)S(1)} %copy-done, f32[1024,256]{1,0:T(8,128)S(1)} %get-tuple-element.6, f32[256]{0:T(256)S(1)} %bitcast.86), kind=kOutput, calls=%fused_computation.26 | convolution fusion | flops 6442713088 | bytes 22021120 | tf_op jit(solution)/shard_map/dot_general | solution.py:17
  299.6 38.2 %shard_map.53 = f32[256,256]{1,0:T(8,128)S(1)} custom-call(f32[256,256]{1,0:T(8,128)S(1)} %fusion.14.refs_0_), custom_call_target="tpu_custom_call" | custom-call | flops 65536 | bytes 2621440 | tf_op jit(solution)/shard_map/pallas_call | solution.py:83
  337.9 11.7 %cholesky.164 = f32[128,128]{1,0:T(8,128)S(1)} custom-call(f32[128,128]{1,0:T(8,128)S(1)} %cholesky.197), custom_call_target="Cholesky" | custom-call | tf_op jit(solution)/shard_map/jit(cholesky)/cholesky | solution.py:120
  349.7 9.8 %custom-call.15 = f32[1,128,128]{1,2,0:T(8,128)S(1)} custom-call(f32[1,128,128]{2,1,0:T(8,128)S(1)} %get-tuple-element.47), custom_call_target="InvertDiagBlocksLowerTriangular" | custom-call | tf_op jit(solution)/shard_map/jit(cholesky)/cholesky | solution.py:120
  360.0 11.9 %cholesky.181 = f32[128,128]{1,0:T(8,128)S(1)} custom-call(f32[128,128]{1,0:T(8,128)S(1)} %convolution_subtract_fusion.2), custom_call_target="Cholesky" | custom-call | tf_op jit(solution)/shard_map/jit(cholesky)/cholesky | solution.py:120
  378.4 19.7 %custom-call.16 = f32[2,128,128]{1,2,0:T(8,128)S(1)} custom-call(f32[2,128,128]{2,1,0:T(8,128)S(1)} %get-tuple-element.23), custom_call_target="InvertDiagBlocksLowerTriangular" | custom-call | tf_op jit(solution)/shard_map/jit(_solve_triangular)/triangular_solve | solution.py:121
  403.4 53.2 %all-reduce.8.cloned.1.call-done = f32[4096,256]{1,0:T(8,128)} async-done(((f32[4096,256]{1,0:T(8,128)}), f32[4096,256]{1,0:T(8,128)}) %all-reduce.8.cloned.1.call-update) | async-done | bytes 4194320 | tf_op jit(solution)/shard_map/psum | solution.py:117
  456.6 5.3 %multiply_reduce_fusion = (f32[256]{0:T(256)S(1)}, f32[4096,256]{1,0:T(8,128)S(1)}) fusion(f32[4096,256]{1,0:T(8,128)} %all-reduce.8.cloned.1.call-done, f32[128,256]{1,0:T(8,128)S(1)} %fusion.32, f32[128,256]{1,0:T(8,128)S(1)} %fusion.27), kind=kOutput, calls=%fused_computation.13 | convolution fusion | flops 3223387904 | bytes 8651776 | tf_op jit(solution)/shard_map/dot_general | solution.py:17
  463.1 8.5 %shard_map.54 = f32[32,256]{1,0:T(8,128)S(1)} custom-call(f32[32,256]{1,0:T(8,128)S(1)} %pad.9.refs_0_), custom_call_target="tpu_custom_call" | custom-call | flops 8192 | bytes 327680 | tf_op jit(solution)/shard_map/pallas_call | solution.py:83
  471.6 14.3 %multiply_subtract_fusion = f32[1024,4096]{1,0:T(8,128)} fusion(f32[1024,4096]{1,0:T(8,128)} %convert_add_fusion, f32[4096,256]{1,0:T(8,128)S(1)} %get-tuple-element.59, f32[1024,256]{0,1:T(8,128)S(1)} %fusion.12), kind=kOutput, calls=%fused_computation.6 | convolution fusion | flops 2157182976 | bytes 38797312 | tf_op jit(solution)/shard_map/dot_general | solution.py:17
  488.2 28.7 %multiply_convert_fusion = bf16[1024,4096]{1,0:T(8,128)(2,1)} fusion(f32[4096,256]{1,0:T(8,128)S(1)} %broadcast_multiply_fusion, f32[4096,256]{1,0:T(8,128)S(1)} %copy-done.1, f32[1024,256]{0,1:T(8,128)S(1)} %fusion.12, f32[1024,256]{0,1:T(8,128)S(1)} %fusion.26), kind=kOutput, calls=%fused_computation.7 | convolution fusion | flops 12895911936 | bytes 18874368 | tf_op jit(solution)/shard_map/dot_general | solution.py:17
  (64 shorter events, 33.8 us)
Async XLA Ops:
  7.2 216.2 %all-reduce.6.cloned.1.call-start = ((), (), s32[]{:S(2)}) async-start(), calls=%async_computation | async-start | bytes 8388608 | tf_op jit(solution)/shard_map/psum | solution.py:117
  61.8 394.8 %all-reduce.8.cloned.1.call-start = ((), (), s32[]{:S(2)}) async-start(), calls=%async_computation.1 | async-start | bytes 8388608 | tf_op jit(solution)/shard_map/psum | solution.py:117
  248.8 33.3 %copy-start = (f32[1024,4096]{1,0:T(8,128)S(1)}, f32[1024,4096]{1,0:T(8,128)}, u32[]{:S(2)}) copy-start(f32[1024,4096]{1,0:T(8,128)} %convert_add_fusion) | copy-start | bytes 50331652
  486.0 2.2 copy-start.1
Sparse Core Ops, SparseCore 0:
  61.9 161.4 all-reduce.5
  297.8 158.7 all-reduce.7

commit v2 on v1

--- a/solution.py
+++ b/solution.py
@@ -17,7 +17,8 @@
     return lax.dot_general(a, b, (dims, ((), ())), precision=precision, preferred_element_type=jnp.float32)
 
 
-def reduce_kernel(axis, bits, count, *refs):
+def reduce_kernel(axis, orders, count, *refs):
+    bits = range(len(orders[0]))
     inputs, outs, recvs, works = (refs[k * count : (k + 1) * count] for k in range(4))
     send_sem, recv_sem = refs[4 * count :]
     me = lax.axis_index(axis)
@@ -35,13 +36,13 @@
             size = inputs[i].shape[0] >> (s + 1)
             base = inputs[i].shape[0] - 2 * size
             source = inputs[i] if s == 0 else works[i]
-            there = pl.multiple_of(starts[i][s] + (1 - halves[s]) * size, 8)
+            there = pl.multiple_of(starts[i][s] + (1 - halves[orders[i][s]]) * size, 8)
             copy = pltpu.make_async_remote_copy(
                 src_ref=source.at[pl.ds(there, size)],
                 dst_ref=recvs[i].at[pl.ds(base, size)],
                 send_sem=send_sem.at[i, s],
                 recv_sem=recv_sem.at[i, s],
-                device_id={axis: partners[s]},
+                device_id={axis: partners[orders[i][s]]},
                 device_id_type=pl.DeviceIdType.MESH,
             )
             copy.start()
@@ -50,7 +51,7 @@
             size = inputs[i].shape[0] >> (s + 1)
             base = inputs[i].shape[0] - 2 * size
             source = inputs[i] if s == 0 else works[i]
-            here = pl.multiple_of(starts[i][s] + halves[s] * size, 8)
+            here = pl.multiple_of(starts[i][s] + halves[orders[i][s]] * size, 8)
             copies[i].wait()
             target = outs[i] if s == len(bits) - 1 else works[i]
             target[pl.ds(here, size), :] = source[pl.ds(here, size), :] + recvs[i][pl.ds(base, size), :]
@@ -66,7 +67,7 @@
                 dst_ref=mine,
                 send_sem=send_sem.at[i, t],
                 recv_sem=recv_sem.at[i, t],
-                device_id={axis: partners[s]},
+                device_id={axis: partners[orders[i][s]]},
                 device_id_type=pl.DeviceIdType.MESH,
             )
             copy.start()
@@ -78,10 +79,11 @@
 def all_reduce(arrays, axis, size, collective_id):
     bits = list(range(size.bit_length() - 1))
     count = len(arrays)
+    orders = [bits[t:] + bits[:t] for t in (min(1, max(0, i - 1)) for i in range(count))]
     total = sum(a.size for a in arrays)
     vmem = pl.BlockSpec(memory_space=pltpu.VMEM)
     return pl.pallas_call(
-        functools.partial(reduce_kernel, axis, bits, count),
+        functools.partial(reduce_kernel, axis, orders, count),
         out_shape=[jax.ShapeDtypeStruct(a.shape, a.dtype) for a in arrays],
         in_specs=[vmem] * count,
         out_specs=[vmem] * count,
@@ -102,7 +104,8 @@
     right = basis
     scale = None
     squares = None
-    lefts, rights = [], []
+    left = None
+    change = 0.0
     steps = grads.shape[0]
     for step in range(steps):
         buffer = state + grads[step].astype(jnp.float32)
@@ -113,23 +116,28 @@
             projected, squares = all_reduce([partial_value, squares], "col", col_size, 1)
             scale = lax.rsqrt(squares[:1] + norm_eps)
             projected = projected * scale
-            rights.append(right * scale)
-        product = lax.psum(matmul(buffer, projected, ((0,), (0,)), HIGH), "row")
+            change = change + factor * matmul(left, right * scale, ((1,), (1,)), HIGH)
+        local = matmul(buffer, projected, ((0,), (0,)), HIGH)
+        eighth = local.shape[0] // 8
+        product = lax.psum(local[: 6 * eighth], "row")
         part = matmul(projected, projected, ((0,), (0,)), HIGHEST)
-        (gram,) = all_reduce([part], "row", row_size, 2)
+        gram, sixth, seventh = all_reduce(
+            [part, local[6 * eighth : 7 * eighth], local[7 * eighth :]], "row", row_size, 2
+        )
+        product = jnp.concatenate([product, sixth, seventh])
         lower = jnp.linalg.cholesky(gram)
         inverse = jax.scipy.linalg.solve_triangular(lower, eye, lower=True)
         ortho = matmul(projected, inverse, ((1,), (1,)), HIGHEST)
-        raw = matmul(product, inverse, ((1,), (1,)), HIGHEST)
-        lefts.append(ortho)
+        raw = matmul(product, inverse, ((1,), (1,)), HIGH)
+        left = ortho
         squares = jnp.pad(jnp.sum(raw * raw, axis=0, keepdims=True), ((0, 8 * col_size - 1), (0, 0)))
         right = raw
         state = buffer - (1.0 - keep_rate) * matmul(
             ortho.astype(jnp.bfloat16), raw.astype(jnp.bfloat16), ((1,), (1,)), None
         )
     (squares,) = all_reduce([squares], "col", col_size, 3)
-    rights.append(right * lax.rsqrt(squares[:1] + norm_eps))
-    change = factor * matmul(jnp.concatenate(lefts, 1), jnp.concatenate(rights, 1), ((1,), (1,)), HIGH)
+    scale = lax.rsqrt(squares[:1] + norm_eps)
+    change = change + factor * matmul(left, right * scale, ((1,), (1,)), HIGH)
     return (change.astype(jnp.bfloat16), state)
 
 

time: 532 us -> 503 us (0.945)
  waiting for transfers between devices: 111 us -> 4.38 us
  Pallas kernels: 128 us -> 209 us
  local copies, waits for them, and re-layouts: 9.94 us -> 19.7 us
  matrix products: 144 us -> 136 us
    psum x2, waiting for transfers between devices: 111 us -> 4.34 us  [shards(): product = lax.psum(local[:6 * eighth], 'row')]
    pallas_call x5, Pallas kernels: 128 us -> 209 us  [all_reduce(): pl.pallas_call(functools.partial(reduce_kernel, axis, orders, count), out...]
    dot_general x13 -> x14, matrix products: 141 us -> 133 us  [matmul(): lax.dot_general(a, b, (dims, ((), ())), precision=precision, preferred_el...]
    slice x0 -> x4, local copies, waits for them, and re-layouts: none -> 8.2 us  [the longest x2 5.66 us: shards(): product = lax.psum(local[:6 * eighth], 'row')]
  transfers between devices with their start and end apart: 2 -> 2, of which waited for: 2 -> 1; matrix products, arithmetic and copies ran while one was open for 25% -> 27% of each run, Pallas kernels for 15% -> 32%
where the time goes in v2:
time: 503 us; the launch traced here: 495 us
  Pallas kernels  209 us (42%)
  matrix products  136 us (27%)
  other arithmetic  109 us (22%)
  local copies, waits for them, and re-layouts  19.7 us (4%)
  between operations  17.4 us (3%)
    pallas_call x5, Pallas kernels, all_reduce(): pl.pallas_call(functools.partial(reduce_kernel, axis, orders, count), out...  209 us
    dot_general x14, matrix products, matmul(): lax.dot_general(a, b, (dims, ((), ())), precision=precision, preferred_el...  133 us
    another operation x13, other arithmetic, shards(): lower = jnp.linalg.cholesky(gram)  69 us
    another operation x5, other arithmetic, shards(): inverse = jax.scipy.linalg.solve_triangular(lower, eye, lower=True)  39.7 us
  transfers between devices with their start and end apart: 2, of which 1 were waited for; matrix products, arithmetic and copies ran while one was open for 27% of the time, Pallas kernels for 32%

profile of v2, /device:TPU:0, one launch (start us, length us, event | category | flops | bytes accessed | tf_op | source)
XLA Modules:
  0.0 495.4 jit_solution(13324094931364409544)
XLA Ops:
  7.2 13.2 %fusion.1.refs_0_ = f32[1024,256]{1,0:T(8,128)S(1)} fusion(f32[4096,256]{1,0:T(8,128)} %param.8, f32[1024,4096]{1,0:T(8,128)} %param.6, bf16[2,1024,4096]{2,1,0:T(8,128)(2,1)} %param.7), kind=kOutput, calls=%fused_computation.9 | convolution fusion | flops 6450839552 | bytes 30408704 | tf_op jit(solution)/shard_map/dot_general | solution.py:17
  20.4 21.3 %shard_map.50 = f32[1024,256]{1,0:T(8,128)S(1)} custom-call(f32[1024,256]{1,0:T(8,128)S(1)} %fusion.1.refs_0_), custom_call_target="tpu_custom_call" | custom-call | flops 262144 | bytes 10485760 | tf_op jit(solution)/shard_map/pallas_call | solution.py:85
  41.8 18.7 %fusion = f32[4096,256]{1,0:T(8,128)S(1)} fusion(f32[1024,256]{1,0:T(8,128)S(1)} %shard_map.50, f32[1024,4096]{1,0:T(8,128)} %param.6, bf16[2,1024,4096]{2,1,0:T(8,128)(2,1)} %param.7), kind=kOutput, calls=%fused_computation.8 | convolution fusion | flops 6450839552 | bytes 30408704 | tf_op jit(solution)/shard_map/dot_general | solution.py:17
  67.8 80.2 %shard_map.51 = (f32[256,256]{1,0:T(8,128)S(1)}, f32[512,256]{1,0:T(8,128)S(1)}, f32[512,256]{1,0:T(8,128)S(1)}) custom-call(f32[256,256]{1,0:T(8,128)S(1)} %fusion.58.refs_0_, f32[512,256]{1,0:T(8,128)S(1)} %get-tuple-element.59.refs_1_, f32[512,256]{1,0:T(8,128)S(1)} %get-tuple-element.58.refs_2_), custom_call_target="tpu_custom_call" | custom-call | flops 327680 | bytes 13107200 | tf_op jit(solution)/shard_map/pallas_call | solution.py:85
  148.2 11.7 %cholesky.130 = f32[128,128]{1,0:T(8,128)S(1)} custom-call(f32[128,128]{1,0:T(8,128)S(1)} %cholesky.194), custom_call_target="Cholesky" | custom-call | tf_op jit(solution)/shard_map/jit(cholesky)/cholesky | solution.py:128
  159.9 9.8 %custom-call.13 = f32[1,128,128]{1,2,0:T(8,128)S(1)} custom-call(f32[1,128,128]{2,1,0:T(8,128)S(1)} %get-tuple-element.67), custom_call_target="InvertDiagBlocksLowerTriangular" | custom-call | tf_op jit(solution)/shard_map/jit(cholesky)/cholesky | solution.py:128
  170.3 12.1 %cholesky.147 = f32[128,128]{1,0:T(8,128)S(1)} custom-call(f32[128,128]{1,0:T(8,128)S(1)} %convolution_subtract_fusion.3), custom_call_target="Cholesky" | custom-call | tf_op jit(solution)/shard_map/jit(cholesky)/cholesky | solution.py:128
  188.0 19.7 %custom-call.14 = f32[2,128,128]{1,2,0:T(8,128)S(1)} custom-call(f32[2,128,128]{2,1,0:T(8,128)S(1)} %get-tuple-element.34), custom_call_target="InvertDiagBlocksLowerTriangular" | custom-call | tf_op jit(solution)/shard_map/jit(_solve_triangular)/triangular_solve | solution.py:129
  210.3 4.3 all-reduce.6.cloned.1.call-done
  214.7 5.7 %multiply_reduce_fusion.1 = (f32[256]{0:T(256)S(1)}, f32[4096,256]{1,0:T(8,128)}) fusion(f32[128,256]{1,0:T(8,128)} %copy-done.5, f32[128,256]{1,0:T(8,128)S(1)} %fusion.38, f32[512,256]{1,0:T(8,128)S(1)} %get-tuple-element.14, f32[512,256]{1,0:T(8,128)S(1)} %get-tuple-element.13, f32[3072,256]{1,0:T(8,128)} %all-reduce.6.cloned.1.call-done), kind=kOutput, calls=%fused_computation.26 | convolution fusion | flops 1614872320 | bytes 8651776 | tf_op jit(solution)/shard_map/dot_general | solution.py:17
  220.4 17.7 %convert_add_fusion = f32[1024,4096]{1,0:T(8,128)} fusion(bf16[2,1024,4096]{2,1,0:T(8,128)(2,1)} %param.7, f32[1024,4096]{1,0:T(8,128)} %param.6, f32[4096,256]{1,0:T(8,128)} %get-tuple-element.71, f32[1024,256]{1,0:T(8,128)S(1)} %fusion.35), kind=kOutput, calls=%fused_computation.4 | convolution fusion | flops 2173960192 | bytes 55574528 | tf_op jit(solution)/shard_map/dot_general | solution.py:17
  238.1 12.6 %fusion.59.refs_0_ = f32[1024,256]{1,0:T(8,128)S(1)} fusion(f32[1024,4096]{1,0:T(8,128)} %convert_add_fusion, f32[4096,256]{1,0:T(8,128)} %get-tuple-element.71), kind=kOutput, calls=%fused_computation.104 | convolution fusion | flops 6442450944 | bytes 22020096 | tf_op jit(solution)/shard_map/dot_general | solution.py:17
  250.8 20.3 %shard_map.52 = (f32[1024,256]{1,0:T(8,128)S(1)}, f32[32,256]{1,0:T(8,128)S(1)}) custom-call(f32[1024,256]{1,0:T(8,128)S(1)} %fusion.59.refs_0_, f32[32,256]{1,0:T(8,128)S(1)} %pad.8.refs_1_), custom_call_target="tpu_custom_call" | custom-call | flops 270336 | bytes 10813440 | tf_op jit(solution)/shard_map/pallas_call | solution.py:85
  272.9 15.6 %fusion.23 = f32[4096,256]{1,0:T(8,128)} fusion(f32[1024,4096]{1,0:T(8,128)S(1)} %copy-done.2, f32[1024,256]{1,0:T(8,128)S(1)} %get-tuple-element.16, f32[256]{0:T(256)S(1)} %bitcast.87), kind=kOutput, calls=%fused_computation.37 | convolution fusion | flops 6442713088 | bytes 22021120 | tf_op jit(solution)/shard_map/dot_general | solution.py:17
  293.7 78.8 %shard_map.53 = (f32[256,256]{1,0:T(8,128)S(1)}, f32[512,256]{1,0:T(8,128)S(1)}, f32[512,256]{1,0:T(8,128)S(1)}) custom-call(f32[256,256]{1,0:T(8,128)S(1)} %fusion.25.refs_0_, f32[512,256]{1,0:T(8,128)S(1)} %get-tuple-element.57.refs_1_, f32[512,256]{1,0:T(8,128)S(1)} %get-tuple-element.56.refs_2_), custom_call_target="tpu_custom_call" | custom-call | flops 327680 | bytes 13107200 | tf_op jit(solution)/shard_map/pallas_call | solution.py:85
  373.5 11.7 %cholesky.164 = f32[128,128]{1,0:T(8,128)S(1)} custom-call(f32[128,128]{1,0:T(8,128)S(1)} %cholesky.197), custom_call_target="Cholesky" | custom-call | tf_op jit(solution)/shard_map/jit(cholesky)/cholesky | solution.py:128
  385.2 9.8 %custom-call.15 = f32[1,128,128]{1,2,0:T(8,128)S(1)} custom-call(f32[1,128,128]{2,1,0:T(8,128)S(1)} %get-tuple-element.63), custom_call_target="InvertDiagBlocksLowerTriangular" | custom-call | tf_op jit(solution)/shard_map/jit(cholesky)/cholesky | solution.py:128
  395.5 11.7 %cholesky.181 = f32[128,128]{1,0:T(8,128)S(1)} custom-call(f32[128,128]{1,0:T(8,128)S(1)} %convolution_subtract_fusion.2), custom_call_target="Cholesky" | custom-call | tf_op jit(solution)/shard_map/jit(cholesky)/cholesky | solution.py:128
  410.0 4.1 while.5
  414.0 19.9 %custom-call.16 = f32[2,128,128]{1,2,0:T(8,128)S(1)} custom-call(f32[2,128,128]{2,1,0:T(8,128)S(1)} %get-tuple-element.35), custom_call_target="InvertDiagBlocksLowerTriangular" | custom-call | tf_op jit(solution)/shard_map/jit(_solve_triangular)/triangular_solve | solution.py:129
  434.9 12.1 %fusion.15 = f32[1024,4096]{1,0:T(8,128)} fusion(f32[1024,256]{1,0:T(8,128)} %copy-done.4, f32[4096,256]{1,0:T(8,128)} %get-tuple-element.71, f32[256]{0:T(256)S(1)} %bitcast.88), kind=kOutput, calls=%fused_computation.24 | convolution fusion | flops 6443499520 | bytes 22021120 | tf_op jit(solution)/shard_map/dot_general | solution.py:17
  451.8 8.5 %shard_map.54 = f32[32,256]{1,0:T(8,128)S(1)} custom-call(f32[32,256]{1,0:T(8,128)S(1)} %pad.9.refs_0_), custom_call_target="tpu_custom_call" | custom-call | flops 8192 | bytes 327680 | tf_op jit(solution)/shard_map/pallas_call | solution.py:85
  460.3 14.3 %multiply_subtract_fusion = f32[1024,4096]{1,0:T(8,128)} fusion(f32[1024,4096]{1,0:T(8,128)} %convert_add_fusion, f32[4096,256]{1,0:T(8,128)S(1)} %get-tuple-element.75, f32[1024,256]{1,0:T(8,128)S(1)} %fusion.21), kind=kOutput, calls=%fused_computation.7 | convolution fusion | flops 2157182976 | bytes 38797312 | tf_op jit(solution)/shard_map/dot_general | solution.py:17
  474.6 13.4 %multiply_convert_fusion = bf16[1024,4096]{1,0:T(8,128)(2,1)} fusion(f32[1024,4096]{1,0:T(8,128)} %fusion.15, f32[1024,256]{1,0:T(8,128)S(1)} %fusion.21, f32[4096,256]{1,0:T(8,128)S(1)} %get-tuple-element.75, f32[256]{0:T(256)S(1)} %bitcast.92), kind=kOutput, calls=%fused_computation.6 | convolution fusion | flops 6456082432 | bytes 30409728 | tf_op jit(solution)/shard_map/dot_general | solution.py:17
  (75 shorter events, 38.2 us)
Async XLA Ops:
  7.2 207.5 %all-reduce.6.cloned.1.call-start = ((), (), s32[]{:S(2)}) async-start(), calls=%async_computation | async-start | bytes 6291456 | tf_op jit(solution)/shard_map/psum | solution.py:122
  60.5 2.0 copy-start.3
  64.4 382.5 %all-reduce.8.cloned.1.call-start = ((), (), s32[]{:S(2)}) async-start(), calls=%async_computation.1 | async-start | bytes 6291456 | tf_op jit(solution)/shard_map/psum | solution.py:122
  208.6 0.6 copy-start.5
  210.3 10.1 %copy-start.4 = (f32[1024,256]{1,0:T(8,128)}, f32[1024,256]{1,0:T(8,128)S(1)}, u32[]{:S(2)}) copy-start(f32[1024,256]{1,0:T(8,128)S(1)} %fusion.35) | copy-start | bytes 3145732
  238.1 34.8 %copy-start.2 = (f32[1024,4096]{1,0:T(8,128)S(1)}, f32[1024,4096]{1,0:T(8,128)}, u32[]{:S(2)}) copy-start(f32[1024,4096]{1,0:T(8,128)} %convert_add_fusion) | copy-start | bytes 50331652
  372.5 0.8 copy-start
  434.9 12.1 %copy-start.1 = (f32[512,256]{1,0:T(8,128)S(1)}, f32[512,256]{1,0:T(8,128)}, u32[]{:S(2)}) copy-start(f32[512,256]{1,0:T(8,128)} %copy-done) | copy-start | bytes 1572868
Sparse Core Ops, SparseCore 0:
  64.6 150.0 all-reduce.5
  293.8 149.2 all-reduce.7
